TPU v7x, 256 devices: a whole 4x4x8 slice. The times are simulated.
256 devices in a mesh: expert: 32 (over x, z), tensor: 8 (over y, core).
Axes of the slice: x: 4, y: 4, z: 8, core: 2. Of those that a mesh axis runs over, the one named last changes fastest.
Arguments:
- tokens: bfloat16 [8192, 4096], P('expert'), may hold values from -6 to 6
- cotangent: bfloat16 [8192, 4096], P('expert'), may hold values from -1.5 to 1.5
- w_in: bfloat16 [4096, 65536], P(None, ('expert', 'tensor')), may hold values from -0.09375 to 0.09375
- w_out: bfloat16 [65536, 4096], P(('expert', 'tensor')), may hold values from -0.09375 to 0.09375
- router: bfloat16 [4096, 16], replicated, may hold values from -0.09375 to 0.09375
- chosen: int32 [16, 512], replicated, may hold values from 0 to 8191, as said below
Outputs:
- grad_tokens: bfloat16 [8192, 4096], P('expert', 'tensor')
- grad_in: bfloat16 [4096, 65536], P(None, ('expert', 'tensor'))
- grad_out: bfloat16 [65536, 4096], P(('expert', 'tensor'))
- grad_router: float32 [4096, 16], replicated
Inputs may be any that keep to these rules, and one draw needn't show every extreme that they name: Row e lists, in increasing order, 512 distinct tokens chosen by expert e; at most 32 of them lie among one device's 256 consecutive tokens, and in every row some device's tokens hold exactly 32 of them.
All inputs are finite; a program needn't handle non-finite values.
Results may differ from a plain program's by a relative error of at most 0.005.
Values may be sent and summed in bfloat16 or wider, within the bound.
A program may use at most 128 MiB of HBM per device.

v0:
```python
import jax
import jax.numpy as jnp
from jax import lax
from jax.sharding import PartitionSpec as P


def body(tokens, cotangent, w_in, w_out, router, chosen):
    tok_dev, features = tokens.shape
    n_expert = lax.axis_size("expert")
    bucket = 4 * tok_dev // n_expert
    capacity = chosen.shape[1]
    expert_total = router.shape[1]
    device_index = lax.axis_index("expert")
    expert = device_index // 2
    slot_range = jnp.arange(bucket, dtype=jnp.int32)
    first_token = device_index * tok_dev
    starts = jnp.sum((chosen < first_token).astype(jnp.int32), axis=1)
    run_ends = jnp.sum((chosen < first_token + tok_dev).astype(jnp.int32), axis=1)
    counts = run_ends - starts
    positions = jnp.minimum(starts[:, None] + slot_range[None, :], capacity - 1)
    picked = jnp.take_along_axis(chosen, positions, axis=1) - first_token
    filled = slot_range[None, :] < counts[:, None]
    local_rows = jnp.where(filled, picked, 0)
    owner_expert = jnp.arange(n_expert, dtype=jnp.int32) // 2
    send_rows = local_rows[owner_expert].reshape(-1)
    send_filled = filled[owner_expert].reshape(-1)

    def pack(source):
        gathered = jnp.where(send_filled[:, None], source[send_rows], jnp.zeros((), source.dtype))
        return gathered.reshape(n_expert, bucket, source.shape[1])

    got_x, got_y = (
        lax.all_to_all(pack(tokens), "expert", split_axis=0, concat_axis=0, tiled=True),
        lax.all_to_all(pack(cotangent), "expert", split_axis=0, concat_axis=0, tiled=True),
    )
    my_chosen = lax.dynamic_index_in_dim(chosen, expert, 0, keepdims=False)
    home_index = my_chosen // tok_dev
    bounds = jnp.arange(n_expert, dtype=jnp.int32) * tok_dev
    run_start = jnp.sum((my_chosen[None, :] < bounds[:, None]).astype(jnp.int32), axis=1)
    slot_index = home_index * bucket + jnp.arange(capacity, dtype=jnp.int32) - run_start[home_index]
    x_rows = got_x.reshape(-1, features)[slot_index]
    grad_rows = got_y.reshape(-1, features)[slot_index]
    r_col = lax.dynamic_slice_in_dim(router, expert, 1, 1)
    gate = jax.nn.sigmoid(jnp.dot(x_rows, r_col, preferred_element_type=jnp.float32)[:, 0])
    pre_act = jnp.dot(x_rows, w_in, preferred_element_type=jnp.float32)
    sig_act = jax.nn.sigmoid(pre_act)
    hidden = pre_act * sig_act
    upstream = jnp.dot(grad_rows, w_out.T, preferred_element_type=jnp.float32)
    gated_hidden = (gate[:, None] * hidden).astype(jnp.bfloat16)
    gate_grad = jnp.sum(hidden * upstream, axis=1)
    pre_grad = (gate[:, None] * upstream * sig_act * (1.0 + pre_act * (1.0 - sig_act))).astype(
        jnp.bfloat16
    )
    grad_out = jnp.dot(gated_hidden.T, grad_rows, preferred_element_type=jnp.float32).astype(
        jnp.bfloat16
    )
    grad_in = jnp.dot(x_rows.T, pre_grad, preferred_element_type=jnp.float32).astype(jnp.bfloat16)
    score_grad = gate_grad * gate * (1.0 - gate)
    router_col = jnp.dot(score_grad, x_rows.astype(jnp.float32), precision=lax.Precision.HIGHEST)
    router_term = (
        router_col[:, None] * (jnp.arange(expert_total) == expert).astype(jnp.float32)[None, :]
    )
    grad_router = lax.psum(router_term, ("expert", "tensor"))
    router_rows = r_col.astype(jnp.float32)
    summed = lax.psum_scatter(
        jnp.dot(w_in, pre_grad.T, preferred_element_type=jnp.float32)
        + router_rows * score_grad[None, :],
        "tensor",
        scatter_dimension=0,
        tiled=True,
    )
    share = summed.shape[0]
    outgoing = jnp.zeros((share, n_expert * bucket), jnp.float32).at[:, slot_index].set(summed)
    returned = lax.all_to_all(
        outgoing.reshape(share, n_expert, bucket), "expert", split_axis=1, concat_axis=1, tiled=True
    )
    returned = jnp.where(send_filled[None, :], returned.reshape(share, -1), 0.0)
    combined = jnp.zeros((share, tok_dev), jnp.float32).at[:, send_rows].add(returned)
    grad_tokens = combined.T.astype(jnp.bfloat16)
    return (grad_tokens, grad_in, grad_out, grad_router)


def solution(mesh):
    placed = (
        P("expert", None),
        P("expert", None),
        P(None, ("expert", "tensor")),
        P(("expert", "tensor"), None),
        P(),
        P(),
    )
    return jax.shard_map(
        body,
        mesh=mesh,
        in_specs=placed,
        out_specs=(
            P("expert", "tensor"),
            P(None, ("expert", "tensor")),
            P(("expert", "tensor"), None),
            P(),
        ),
        check_vma=False,
    )
```

profile of v0, /device:TPU:2, one launch (start us, length us, event | category | flops | bytes accessed | tf_op | source)
XLA Modules:
  0.0 806.7 jit_solution(2339139497223671526)
XLA Ops:
  8.1 1.0 convert_reduce_fusion.2
  9.2 4.5 gather_fusion.6
  15.3 7.8 gather_fusion.4
  23.1 16.9 %gather_fusion.2 = bf16[1024,4096]{1,0:T(8,128)(2,1)} fusion(bf16[256,4096]{1,0:T(8,128)(2,1)} %param.6, s32[1024]{0:T(1024)S(1)} %broadcast_clamp_fusion), kind=kCustom, calls=%fused_computation.2 | custom fusion | bytes 16781312 | tf_op jit(solution)/shard_map/gather | solution.py:29
  40.0 9.2 %broadcast_select_fusion = (bf16[32,32,4096]{2,1,0:T(8,128)(2,1)}, bf16[32,32,4096]{2,1,0:T(8,128)(2,1)S(1)}) fusion(bf16[32,32,4096]{2,1,0:T(8,128)(2,1)} %bitcast.83, pred[32,32]{1,0:T(8,128)(4,1)S(1)} %gather_fusion.1, bf16[32,32,4096]{2,1,0:T(8,128)(2,1)} %bitcast.84), kind=kLoop, calls=%fused_computation.10 | loop fusion | flops 8388608 | bytes 33555456 | tf_op jit(solution)/shard_map/jit(_where)/select_n | solution.py:29
  49.2 194.9 %all_to_all.15 = bf16[32,32,4096]{2,1,0:T(8,128)(2,1)} all-to-all(bf16[32,32,4096]{2,1,0:T(8,128)(2,1)S(1)} %get-tuple-element.37), channel_id=1, replica_groups=mesh['expert'=32,'tensor'=8] {'expert'}, dimensions={0} | all-to-all | bytes 16777216 | tf_op jit(solution)/shard_map/all_to_all | solution.py:33
  244.1 7.7 all-to-all-start.1
  251.9 0.9 dynamic-slice_reduce_fusion
  253.0 0.7 fusion.21
  253.7 4.3 compare_select_fusion.5
  258.1 0.7 fusion.20
  258.9 15.5 %select_select_fusion = s32[512]{0:T(512)S(1)} fusion(pred[512]{0:T(512)(128)(4,1)S(1)} %get-tuple-element.30, pred[512]{0:T(512)(128)(4,1)S(1)} %get-tuple-element.29, pred[512]{0:T(512)(128)(4,1)S(1)} %get-tuple-element.28, pred[512]{0:T(512)(128)(4,1)S(1)} %get-tuple-element.27, pred[512]{0:T(512)(128)(4,1)S(1)} %get-tuple-element.26, ...), kind=kLoop, calls=%fused_computation.88 | loop fusion | flops 12800 | bytes 16996 | tf_op jit(solution)/shard_map/gather | solution.py:40
  274.5 13.3 %gather_fusion.3 = bf16[512,4096]{1,0:T(8,128)(2,1)} fusion(bf16[1024,4096]{1,0:T(8,128)(2,1)} %bitcast.82, s32[1024]{0:T(1024)S(1)} %pad_clamp_fusion), kind=kCustom, calls=%fused_computation.3 | custom fusion | bytes 8390656 | tf_op jit(solution)/shard_map/gather | solution.py:41
  287.9 3.5 fusion.9
  291.4 1.3 fusion.22
  292.7 144.1 %all-to-all-done.1 = bf16[32,32,4096]{2,1,0:T(8,128)(2,1)} async-done(((bf16[32,32,4096]{2,1,0:T(8,128)(2,1)}), bf16[32,32,4096]{2,1,0:T(8,128)(2,1)}, u32[]{:S(2)}, u32[]{:S(2)}) %all-to-all-start.1) | async-done | bytes 8388640 | tf_op jit(solution)/shard_map/all_to_all | solution.py:34
  436.9 13.0 %gather_fusion.5 = bf16[512,4096]{1,0:T(8,128)(2,1)} fusion(bf16[1024,4096]{1,0:T(8,128)(2,1)} %bitcast.43, s32[1024]{0:T(1024)S(1)} %pad_clamp_fusion), kind=kCustom, calls=%fused_computation.5 | custom fusion | bytes 8390656 | tf_op jit(solution)/shard_map/gather | solution.py:42
  449.9 4.3 multiply_reduce_fusion
  454.2 5.1 bitcast_add_fusion
  459.3 57.6 %reduce-scatter.2.cloned.1.call-done = f32[512,512]{0,1:T(8,128)} async-done(((f32[4096,512]{0,1:T(8,128)}), f32[512,512]{0,1:T(8,128)}) %reduce-scatter.2.cloned.1.call-update) | async-done | bytes 1048592 | tf_op jit(solution)/shard_map/reduce_scatter | solution.py:65
  517.0 4.4 scatter_custom_fusion
  521.4 10.2 %all-to-all-start.2 = ((f32[512,32,32]{0,2,1:T(8,128)}), f32[512,32,32]{0,2,1:T(8,128)}, u32[]{:S(2)}, u32[]{:S(2)}) async-start(f32[512,32,32]{0,2,1:T(8,128)} %bitcast.46), calls=%async_computation.3 | async-start | bytes 4194304 | tf_op jit(solution)/shard_map/all_to_all | solution.py:74
  531.7 3.9 fusion.23
  535.6 0.8 broadcast_multiply_fusion
  536.5 5.0 convolution_convert_fusion.1
  541.4 2.6 convolution_convert_fusion
  544.1 34.9 %all-to-all-done.2 = f32[512,32,32]{0,2,1:T(8,128)} async-done(((f32[512,32,32]{0,2,1:T(8,128)}), f32[512,32,32]{0,2,1:T(8,128)}, u32[]{:S(2)}, u32[]{:S(2)}) %all-to-all-start.2) | async-done | bytes 2097184 | tf_op jit(solution)/shard_map/all_to_all | solution.py:74
  579.0 3.2 bitcast_select_fusion
  582.2 7.6 scatter_custom_fusion.1
  589.8 0.7 convert_bitcast_fusion
  590.5 207.0 %all-reduce.2.cloned.1.call-done = f32[4096,16]{0,1:T(8,128)} async-done(((f32[4096,16]{0,1:T(8,128)}), f32[4096,16]{0,1:T(8,128)}) %all-reduce.2.cloned.1.call-update) | async-done | bytes 262160 | tf_op jit(solution)/shard_map/psum | solution.py:63
  797.6 1.7 copy.11
  (40 shorter events, 2.3 us)
Async XLA Ops:
  8.0 7.3 copy-start
  8.0 1.2 copy-start.2
  244.1 192.7 %all-to-all-start.1 = ((bf16[32,32,4096]{2,1,0:T(8,128)(2,1)}), bf16[32,32,4096]{2,1,0:T(8,128)(2,1)}, u32[]{:S(2)}, u32[]{:S(2)}) async-start(bf16[32,32,4096]{2,1,0:T(8,128)(2,1)} %get-tuple-element.36), calls=%async_computation.1 | async-start | bytes 16777216 | tf_op jit(solution)/shard_map/all_to_all | solution.py:34
  251.8 265.1 %reduce-scatter.2.cloned.1.call-start = ((), (), s32[]{:S(2)}) async-start(), calls=%async_computation.4 | async-start | bytes 9437184 | tf_op jit(solution)/shard_map/reduce_scatter | solution.py:65
  274.5 16.9 %copy-start.5 = (bf16[4096,256]{1,0:T(8,128)(2,1)S(1)}, bf16[4096,256]{1,0:T(8,128)(2,1)}, u32[]{:S(2)}) copy-start(bf16[4096,256]{1,0:T(8,128)(2,1)} %param.8) | copy-start | bytes 6291460
  287.9 3.5 copy-start.3
  521.4 57.6 %all-to-all-start.2 = ((f32[512,32,32]{0,2,1:T(8,128)}), f32[512,32,32]{0,2,1:T(8,128)}, u32[]{:S(2)}, u32[]{:S(2)}) async-start(f32[512,32,32]{0,2,1:T(8,128)} %bitcast.46), calls=%async_computation.3 | async-start | bytes 4194304 | tf_op jit(solution)/shard_map/all_to_all | solution.py:74
  531.6 266.0 %all-reduce.2.cloned.1.call-start = ((), (), s32[]{:S(2)}) async-start(), calls=%async_computation.5 | async-start | bytes 524288 | tf_op jit(solution)/shard_map/psum | solution.py:63
  536.5 5.0 copy-start.4
  541.4 257.8 %copy-start.1 = (bf16[256,4096]{1,0:T(8,128)(2,1)S(1)}, bf16[256,4096]{1,0:T(8,128)(2,1)}, u32[]{:S(2)}) copy-start(bf16[256,4096]{1,0:T(8,128)(2,1)} %param.7) | copy-start | bytes 6291460
Sparse Core Ops, SparseCore 0:
  459.4 57.4 reduce-scatter.1
Sparse Core Ops, SparseCore 1:
  538.1 259.4 all-reduce.1
where the time goes:
time: 808 us; the launch traced here: 807 us
  waiting for transfers between devices  444 us (55%)
  blocking collectives  195 us (24%)
  local copies, waits for them, and re-layouts  65.6 us (8%)
  other arithmetic  43 us (5%)
  matrix products  25.8 us (3%)
  starting transfers between devices  18 us (2%)
  between operations  15.7 us (2%)
    psum x1, waiting for transfers between devices, body(): grad_router = lax.psum(router_term, ('expert', 'tensor'))  207 us
    all_to_all x1, blocking collectives, body(): lax.all_to_all(pack(tokens), 'expert', split_axis=0, concat_axis=0, tiled...  195 us
    all_to_all x1, waiting for transfers between devices, body(): lax.all_to_all(pack(cotangent), 'expert', split_axis=0, concat_axis=0, ti...  144 us
    reduce_scatter x1, waiting for transfers between devices, body(): lax.psum_scatter(jnp.dot(w_in, pre_grad.T, preferred_element_type=jnp.flo...  57.6 us
    all_to_all x1, waiting for transfers between devices, body(): lax.all_to_all(outgoing.reshape(share, n_expert, bucket), 'expert', split...  34.9 us
    gather x2, local copies, waits for them, and re-layouts, pack(): source[send_rows]  24.8 us
    gather x3, other arithmetic, body(): run_start[home_index]  20 us
  transfers between devices with their start and end apart: 4, of which 4 were waited for; matrix products, arithmetic and copies ran while one was open for 8% of the time, Pallas kernels for 0%

commit v1 on v0

--- a/solution.py
+++ b/solution.py
@@ -60,7 +60,9 @@
     router_term = (
         router_col[:, None] * (jnp.arange(expert_total) == expert).astype(jnp.float32)[None, :]
     )
-    grad_router = lax.psum(router_term, ("expert", "tensor"))
+    grad_router = router_term
+    for axis in ("expert", "tensor"):
+        grad_router = lax.psum(grad_router, axis)
     router_rows = r_col.astype(jnp.float32)
     summed = lax.psum_scatter(
         jnp.dot(w_in, pre_grad.T, preferred_element_type=jnp.float32)

time: 808 us -> 760 us (0.941)
  waiting for transfers between devices: 444 us -> 396 us
    all_to_all x1, waiting for transfers between devices: 34.9 us -> 0.01 us  [body(): lax.all_to_all(outgoing.reshape(share, n_expert, bucket), 'expert', split...]
    psum x1 -> x2, waiting for transfers between devices: 207 us -> 194 us  [body(): grad_router = lax.psum(grad_router, axis)]
  transfers between devices with their start and end apart: 4 -> 5, of which waited for: 4 -> 4; matrix products, arithmetic and copies ran while one was open for 8% -> 9% of each run, Pallas kernels for 0% -> 0%
where the time goes in v1:
time: 760 us; the launch traced here: 759 us
  waiting for transfers between devices  396 us (52%)
  blocking collectives  195 us (26%)
  local copies, waits for them, and re-layouts  65.6 us (9%)
  other arithmetic  43.2 us (6%)
  matrix products  25.7 us (3%)
  starting transfers between devices  18 us (2%)
  between operations  15.7 us (2%)
    all_to_all x1, blocking collectives, body(): lax.all_to_all(pack(tokens), 'expert', split_axis=0, concat_axis=0, tiled...  195 us
    psum x2, waiting for transfers between devices, body(): grad_router = lax.psum(grad_router, axis)  194 us
    all_to_all x1, waiting for transfers between devices, body(): lax.all_to_all(pack(cotangent), 'expert', split_axis=0, concat_axis=0, ti...  144 us
    reduce_scatter x1, waiting for transfers between devices, body(): lax.psum_scatter(jnp.dot(w_in, pre_grad.T, preferred_element_type=jnp.flo...  57.6 us
    gather x2, local copies, waits for them, and re-layouts, pack(): source[send_rows]  24.8 us
    gather x3, other arithmetic, body(): run_start[home_index]  20 us
  transfers between devices with their start and end apart: 5, of which 4 were waited for; matrix products, arithmetic and copies ran while one was open for 9% of the time, Pallas kernels for 0%

profile of v1, /device:TPU:2, one launch (start us, length us, event | category | flops | bytes accessed | tf_op | source)
XLA Modules:
  0.0 759.1 jit_solution(7239756265299898916)
XLA Ops:
  8.1 1.0 convert_reduce_fusion.2
  9.2 4.5 gather_fusion.6
  15.3 7.8 %gather_fusion.4 = bf16[1024,4096]{1,0:T(8,128)(2,1)} fusion(bf16[256,4096]{1,0:T(8,128)(2,1)S(1)} %copy-done, s32[1024]{0:T(1024)S(1)} %broadcast_clamp_fusion), kind=kCustom, calls=%fused_computation.4 | custom fusion | bytes 16781312 | tf_op jit(solution)/shard_map/gather | solution.py:29
  23.1 16.9 %gather_fusion.2 = bf16[1024,4096]{1,0:T(8,128)(2,1)} fusion(bf16[256,4096]{1,0:T(8,128)(2,1)} %param.6, s32[1024]{0:T(1024)S(1)} %broadcast_clamp_fusion), kind=kCustom, calls=%fused_computation.2 | custom fusion | bytes 16781312 | tf_op jit(solution)/shard_map/gather | solution.py:29
  40.0 9.2 %broadcast_select_fusion = (bf16[32,32,4096]{2,1,0:T(8,128)(2,1)}, bf16[32,32,4096]{2,1,0:T(8,128)(2,1)S(1)}) fusion(bf16[32,32,4096]{2,1,0:T(8,128)(2,1)} %bitcast.83, pred[32,32]{1,0:T(8,128)(4,1)S(1)} %gather_fusion.1, bf16[32,32,4096]{2,1,0:T(8,128)(2,1)} %bitcast.84), kind=kLoop, calls=%fused_computation.10 | loop fusion | flops 8388608 | bytes 33555456 | tf_op jit(solution)/shard_map/jit(_where)/select_n | solution.py:29
  49.2 194.9 %all_to_all.15 = bf16[32,32,4096]{2,1,0:T(8,128)(2,1)} all-to-all(bf16[32,32,4096]{2,1,0:T(8,128)(2,1)S(1)} %get-tuple-element.37), channel_id=1, replica_groups=mesh['expert'=32,'tensor'=8] {'expert'}, dimensions={0} | all-to-all | bytes 16777216 | tf_op jit(solution)/shard_map/all_to_all | solution.py:33
  244.1 7.7 %all-to-all-start.1 = ((bf16[32,32,4096]{2,1,0:T(8,128)(2,1)}), bf16[32,32,4096]{2,1,0:T(8,128)(2,1)}, u32[]{:S(2)}, u32[]{:S(2)}) async-start(bf16[32,32,4096]{2,1,0:T(8,128)(2,1)} %get-tuple-element.36), calls=%async_computation.1 | async-start | bytes 16777216 | tf_op jit(solution)/shard_map/all_to_all | solution.py:34
  251.9 0.9 dynamic-slice_reduce_fusion
  253.0 0.7 fusion.21
  253.7 4.3 compare_select_fusion.5
  258.1 0.7 fusion.20
  258.9 15.5 %select_select_fusion = s32[512]{0:T(512)S(1)} fusion(pred[512]{0:T(512)(128)(4,1)S(1)} %get-tuple-element.30, pred[512]{0:T(512)(128)(4,1)S(1)} %get-tuple-element.29, pred[512]{0:T(512)(128)(4,1)S(1)} %get-tuple-element.28, pred[512]{0:T(512)(128)(4,1)S(1)} %get-tuple-element.27, pred[512]{0:T(512)(128)(4,1)S(1)} %get-tuple-element.26, ...), kind=kLoop, calls=%fused_computation.88 | loop fusion | flops 12800 | bytes 16996 | tf_op jit(solution)/shard_map/gather | solution.py:40
  274.5 13.3 %gather_fusion.3 = bf16[512,4096]{1,0:T(8,128)(2,1)} fusion(bf16[1024,4096]{1,0:T(8,128)(2,1)} %bitcast.82, s32[1024]{0:T(1024)S(1)} %pad_clamp_fusion), kind=kCustom, calls=%fused_computation.3 | custom fusion | bytes 8390656 | tf_op jit(solution)/shard_map/gather | solution.py:41
  287.9 3.5 fusion.9
  291.4 1.3 fusion.22
  292.7 144.1 %all-to-all-done.1 = bf16[32,32,4096]{2,1,0:T(8,128)(2,1)} async-done(((bf16[32,32,4096]{2,1,0:T(8,128)(2,1)}), bf16[32,32,4096]{2,1,0:T(8,128)(2,1)}, u32[]{:S(2)}, u32[]{:S(2)}) %all-to-all-start.1) | async-done | bytes 8388640 | tf_op jit(solution)/shard_map/all_to_all | solution.py:34
  436.9 13.0 %gather_fusion.5 = bf16[512,4096]{1,0:T(8,128)(2,1)} fusion(bf16[1024,4096]{1,0:T(8,128)(2,1)} %bitcast.43, s32[1024]{0:T(1024)S(1)} %pad_clamp_fusion), kind=kCustom, calls=%fused_computation.5 | custom fusion | bytes 8390656 | tf_op jit(solution)/shard_map/gather | solution.py:42
  449.9 4.3 multiply_reduce_fusion
  454.2 5.1 bitcast_add_fusion
  459.3 57.6 %reduce-scatter.2.cloned.1.call-done = f32[512,512]{0,1:T(8,128)} async-done(((f32[4096,512]{0,1:T(8,128)}), f32[512,512]{0,1:T(8,128)}) %reduce-scatter.2.cloned.1.call-update) | async-done | bytes 1048592 | tf_op jit(solution)/shard_map/reduce_scatter | solution.py:67
  517.0 4.4 scatter_custom_fusion
  521.4 10.2 %all-to-all-start.2 = ((f32[512,32,32]{0,2,1:T(8,128)}), f32[512,32,32]{0,2,1:T(8,128)}, u32[]{:S(2)}, u32[]{:S(2)}) async-start(f32[512,32,32]{0,2,1:T(8,128)} %bitcast.46), calls=%async_computation.3 | async-start | bytes 4194304 | tf_op jit(solution)/shard_map/all_to_all | solution.py:76
  531.7 3.9 fusion.23
  535.6 0.8 broadcast_multiply_fusion
  536.5 4.9 convolution_convert_fusion
  541.5 2.6 convolution_convert_fusion.1
  544.1 142.0 %all-reduce.3.cloned.1.call-done = f32[4096,16]{0,1:T(8,128)} async-done(((f32[4096,16]{0,1:T(8,128)}), f32[4096,16]{0,1:T(8,128)}) %all-reduce.3.cloned.1.call-update) | async-done | bytes 262160 | tf_op jit(solution)/shard_map/psum | solution.py:65
  686.1 3.3 bitcast_select_fusion
  689.4 7.6 %scatter_custom_fusion.1 = f32[512,256]{0,1:T(8,128)S(1)} fusion(s32[1024]{0:T(1024)S(1)} %bitcast.90, f32[512,1024]{0,1:T(8,128)} %bitcast_select_fusion, f32[]{:T(128)} %constant.70.clone.1), kind=kCustom, calls=%fused_computation.14 | custom fusion | flops 524288 | bytes 2621444 | tf_op jit(solution)/shard_map/scatter-add | solution.py:80
  697.1 0.7 convert_bitcast_fusion
  697.8 52.2 %all-reduce.5.cloned.1.call-done = f32[4096,16]{0,1:T(8,128)} async-done(((f32[4096,16]{0,1:T(8,128)}), f32[4096,16]{0,1:T(8,128)}) %all-reduce.5.cloned.1.call-update) | async-done | bytes 262160 | tf_op jit(solution)/shard_map/psum | solution.py:65
  750.0 1.7 copy.12
  (43 shorter events, 2.4 us)
Async XLA Ops:
  8.0 7.3 copy-start
  8.0 1.2 copy-start.2
  244.1 192.7 %all-to-all-start.1 = ((bf16[32,32,4096]{2,1,0:T(8,128)(2,1)}), bf16[32,32,4096]{2,1,0:T(8,128)(2,1)}, u32[]{:S(2)}, u32[]{:S(2)}) async-start(bf16[32,32,4096]{2,1,0:T(8,128)(2,1)} %get-tuple-element.36), calls=%async_computation.1 | async-start | bytes 16777216 | tf_op jit(solution)/shard_map/all_to_all | solution.py:34
  251.8 265.1 %reduce-scatter.2.cloned.1.call-start = ((), (), s32[]{:S(2)}) async-start(), calls=%async_computation.4 | async-start | bytes 9437184 | tf_op jit(solution)/shard_map/reduce_scatter | solution.py:67
  274.5 16.9 %copy-start.5 = (bf16[4096,256]{1,0:T(8,128)(2,1)S(1)}, bf16[4096,256]{1,0:T(8,128)(2,1)}, u32[]{:S(2)}) copy-start(bf16[4096,256]{1,0:T(8,128)(2,1)} %param.8) | copy-start | bytes 6291460
  287.9 3.5 copy-start.3
  521.4 164.7 %all-to-all-start.2 = ((f32[512,32,32]{0,2,1:T(8,128)}), f32[512,32,32]{0,2,1:T(8,128)}, u32[]{:S(2)}, u32[]{:S(2)}) async-start(f32[512,32,32]{0,2,1:T(8,128)} %bitcast.46), calls=%async_computation.3 | async-start | bytes 4194304 | tf_op jit(solution)/shard_map/all_to_all | solution.py:76
  531.6 154.5 %all-reduce.3.cloned.1.call-start = ((), (), s32[]{:S(2)}) async-start(), calls=%async_computation.5 | async-start | bytes 524288 | tf_op jit(solution)/shard_map/psum | solution.py:65
  536.5 213.6 %all-reduce.5.cloned.1.call-start = ((), (), s32[]{:S(2)}) async-start(), calls=%async_computation.6 | async-start | bytes 524288 | tf_op jit(solution)/shard_map/psum | solution.py:65
  536.5 5.0 copy-start.4
  686.1 65.6 %copy-start.1 = (bf16[256,4096]{1,0:T(8,128)(2,1)S(1)}, bf16[256,4096]{1,0:T(8,128)(2,1)}, u32[]{:S(2)}) copy-start(bf16[256,4096]{1,0:T(8,128)(2,1)} %param.7) | copy-start | bytes 6291460
Sparse Core Ops, SparseCore 0:
  459.4 57.4 reduce-scatter.1
  686.2 63.7 all-reduce.4
Sparse Core Ops, SparseCore 1:
  536.5 149.5 all-reduce.2
